TPU v7x, 256 devices: a whole 4x4x8 slice. The times are simulated.
256 devices in a mesh: layer: 4 (over y), row: 16 (over z, core), col: 4 (over x).
Axes of the slice: x: 4, y: 4, z: 8, core: 2. Of those that a mesh axis runs over, the one named last changes fastest.
Arguments:
- ancestor: float32 [6144, 6144], P('row', 'col'), may hold values from -6 to 6
- leaf_lower: bfloat16 [4, 8, 6144, 512], P('layer', 'col', 'row'), may hold values from -6 to 6
- leaf_upper: bfloat16 [4, 8, 512, 6144], P('layer', None, 'row', 'col'), may hold values from -6 to 6
- leaf_upper_inv: bfloat16 [4, 8, 512, 512], P('layer', 'col'), may hold values from -1 to 1, as said below
- leaf_lower_inv: bfloat16 [4, 8, 512, 512], P('layer'), may hold values from -1 to 2, as said below
- leaf_pivots: int32 [4, 8, 512], P('layer'), may hold values from 0 to 511, each once within a row
- leaf_tiles: int32 [4, 8, 24, 24], P('layer'), may hold values 0 or 1
- anc_upper_inv: bfloat16 [512, 512], replicated, may hold values from -1 to 1, as said below
- anc_lower_inv: bfloat16 [512, 512], replicated, may hold values from -1 to 2, as said below
- anc_pivots: int32 [512], replicated, may hold values from 0 to 511, each once
- anc_tiles: int32 [24, 24], replicated, may hold values 0 or 1
Outputs:
- anc_lower: bfloat16 [6144, 512], P('row')
- anc_upper: bfloat16 [512, 6144], P(None, 'col')
- schur: float32 [6144, 6144], P('row', 'col')
Inputs may be any that keep to these rules, and one draw needn't show every extreme that they name: leaf_upper_inv[l,k] is upper triangular with positive diagonal. leaf_lower_inv[l,k] is lower triangular with positive diagonal. `anc_upper_inv`: upper triangular with positive diagonal. `anc_lower_inv`: lower triangular with positive diagonal.
All inputs are finite; a program needn't handle non-finite values. No bound on the sum of `leaf_tiles` on one device may be relied on, other than what follows from the above.
Results may differ from a plain program's by a relative error of at most 0.0085.
Values may be sent and summed in bfloat16 or wider, within the bound.
A program may use at most 128 MiB of HBM per device.

v0:
```python
import jax
import jax.numpy as jnp
from jax import lax
from jax.sharding import PartitionSpec as P

W = 512
TB = 256
NT = 24


def joined_along(blocks, dim):
    blocks = jnp.moveaxis(blocks, 0, dim)
    lengths = blocks.shape
    return blocks.reshape(*lengths[:dim], lengths[dim] * lengths[dim + 1], *lengths[dim + 2 :])


def sent_to_all(x, axis):
    count = lax.axis_size(axis)
    return lax.all_to_all(jnp.broadcast_to(x[None], (count, *x.shape)), axis, 0, 0, tiled=True)


def gathered_copies(x, axis, dim):
    return joined_along(sent_to_all(x, axis), dim)


def from_root(x, axis, root):
    return lax.dynamic_index_in_dim(lax.all_gather(x, axis), root, 0, keepdims=False)


def onehot_tiles(first, count):
    positions = first + jnp.arange(count, dtype=jnp.int32)
    tile_index = positions // TB
    return (tile_index[:, None] == jnp.arange(NT, dtype=jnp.int32)[None, :]).astype(jnp.float32)


def shards(
    ancestor,
    leaf_lower,
    leaf_upper,
    leaf_upper_inv,
    leaf_lower_inv,
    leaf_pivots,
    leaf_tiles,
    anc_upper_inv,
    anc_lower_inv,
    anc_pivots,
    anc_tiles,
):
    row_count, col_count = ancestor.shape
    panel_rows = leaf_upper.shape[2]
    row_onehot = onehot_tiles(lax.axis_index("row") * row_count, row_count)
    col_onehot = onehot_tiles(lax.axis_index("col") * col_count, col_count)
    upper_local = leaf_upper[0]
    column_share = lax.all_to_all(upper_local, "row", split_axis=2, concat_axis=1, tiled=True)
    permuted = jnp.take_along_axis(column_share, leaf_pivots[0][:, :, None], axis=1)
    finished = jnp.einsum(
        "kij,kjc->kic", leaf_lower_inv[0], permuted, preferred_element_type=jnp.float32
    ).astype(jnp.bfloat16)
    upper_all = lax.all_gather(finished, "row", axis=2, tiled=True)
    own_lower = jnp.einsum(
        "jrw,jwv->jrv", leaf_lower[0], leaf_upper_inv[0], preferred_element_type=jnp.float32
    ).astype(jnp.bfloat16)
    tiles_float = leaf_tiles[0].astype(jnp.float32)
    masks = jnp.einsum("rt,mts,cs->mrc", row_onehot, tiles_float, col_onehot)
    products = jnp.einsum(
        "mrw,mwc->mrc",
        lax.all_gather(own_lower, "col", axis=0, tiled=True),
        upper_all,
        preferred_element_type=jnp.float32,
    )
    contrib = jnp.sum(masks * products, axis=0)
    total = lax.psum(contrib, "layer")
    a_sum = ancestor + total
    local_pivot = a_sum[:panel_rows].astype(jnp.bfloat16)
    gathered = gathered_copies(local_pivot, "row", 0)
    reordered = jnp.take(gathered, anc_pivots, axis=0)
    anc_upper = jnp.dot(anc_lower_inv, reordered, preferred_element_type=jnp.float32).astype(
        jnp.bfloat16
    )
    columns = a_sum[:, :W].astype(jnp.bfloat16)
    panel = jnp.dot(columns, anc_upper_inv, preferred_element_type=jnp.float32).astype(jnp.bfloat16)
    anc_lower = from_root(panel, "col", 0)
    anc_mask = jnp.einsum("rt,ts,cs->rc", row_onehot, anc_tiles.astype(jnp.float32), col_onehot)
    schur = a_sum - anc_mask * jnp.dot(anc_lower, anc_upper, preferred_element_type=jnp.float32)
    return (anc_lower, anc_upper, schur)


def solution(mesh):
    return jax.shard_map(
        shards,
        mesh=mesh,
        in_specs=(
            P("row", "col"),
            P("layer", "col", "row", None),
            P("layer", None, "row", "col"),
            P("layer", "col", None, None),
            P("layer", None, None, None),
            P("layer", None, None),
            P("layer", None, None, None),
            P(),
            P(),
            P(),
            P(),
        ),
        out_specs=(P("row", None), P(None, "col"), P("row", "col")),
        check_vma=False,
    )
```

profile of v0, /device:TPU:1, one launch (start us, length us, event | category | flops | bytes accessed | tf_op | source)
XLA Modules:
  0.0 328.2 jit_solution(1591160123530114196)
XLA Ops:
  7.2 0.0 copy-start
  7.2 0.0 copy-start.6
  7.2 0.0 all-gather.5.cloned.1.call-start
  7.2 1.2 copy-done
  8.4 2.6 convolution_convert_fusion.1
  11.0 0.0 all-gather.5.cloned.1.call-update
  11.0 0.0 copy-done.6
  11.0 3.5 %copy.16 = bf16[1,8,32,1536]{2,1,3,0:T(8,128)(2,1)} copy(bf16[1,8,32,1536]{3,2,1,0:T(8,128)(2,1)S(1)} %copy-done.6) | data formatting | bytes 1572864 | tf_op args[2]
  14.5 3.1 bitcast_bitcast_fusion
  17.6 5.7 %reshape.121 = bf16[16,2,12288]{2,1,0:T(2,128)(2,1)} reshape(bf16[1536,8,32]{2,1,0:T(8,128)(2,1)} %bitcast_bitcast_fusion) | data formatting | bytes 1572864
  23.3 10.0 %all-to-all-start = ((bf16[16,2,12288]{2,1,0:T(2,128)(2,1)}), bf16[16,2,12288]{2,1,0:T(2,128)(2,1)S(1)}, u32[]{:S(2)}, u32[]{:S(2)}) async-start(bf16[16,2,12288]{2,1,0:T(2,128)(2,1)} %reshape.121), calls=%async_computation | async-start | bytes 1572864 | tf_op jit(solution)/shard_map/all_to_all | solution.py:54
  33.3 0.0 all-gather.7.cloned.1.call-start
  33.3 0.0 copy-done.8
  33.4 22.6 %all-to-all-done = bf16[16,2,12288]{2,1,0:T(2,128)(2,1)S(1)} async-done(((bf16[16,2,12288]{2,1,0:T(2,128)(2,1)}), bf16[16,2,12288]{2,1,0:T(2,128)(2,1)S(1)}, u32[]{:S(2)}, u32[]{:S(2)}) %all-to-all-start) | async-done | bytes 786464 | tf_op jit(solution)/shard_map/all_to_all | solution.py:54
  56.0 2.7 reshape.122
  58.7 3.9 %copy.17 = bf16[8,32,16,96]{3,1,2,0:T(8,128)(2,1)S(1)} copy(bf16[8,32,16,96]{1,0,3,2:T(8,128)(2,1)} %bitcast.62) | data formatting | bytes 1572864 | tf_op jit(solution)/shard_map/all_to_all | solution.py:54
  62.6 21.7 %gather_fusion.1 = bf16[4096,96]{1,0:T(8,128)(2,1)S(1)} fusion(bf16[8,512,96]{2,1,0:T(8,128)(2,1)S(1)} %bitcast.61, s32[4096]{0:T(1024)S(1)} %bitcast.59), kind=kCustom, calls=%fused_computation.1 | custom fusion | bytes 1605632 | tf_op jit(solution)/shard_map/jit(take_along_axis)/gather | solution.py:55
  84.3 4.5 %fusion.8 = bf16[8,512,96]{1,2,0:T(8,128)(2,1)} fusion(bf16[1,8,512,512]{3,2,1,0:T(8,128)(2,1)} %param.15, bf16[8,512,96]{2,1,0:T(8,128)(2,1)S(1)} %bitcast.64, pred[8,512]{1,0:T(8,128)(4,1)S(1)} %compare_and_fusion), kind=kOutput, calls=%fused_computation.12 | convolution fusion | flops 403439616 | bytes 5771264 | tf_op jit(solution)/shard_map/kij,kjc->kic/dot_general | solution.py:56
  88.8 0.0 all-gather.7.cloned.1.call-update
  88.8 0.0 all-reduce.2.cloned.1.call-start
  88.9 0.0 copy-start.7
  88.9 0.0 all-gather.5.cloned.1.call-done
  88.9 72.9 %all-gather.7.cloned.1.call-done = bf16[8,512,1536]{1,2,0:T(8,128)(2,1)} async-done(((bf16[8,512,96]{1,2,0:T(8,128)(2,1)}), bf16[8,512,1536]{1,2,0:T(8,128)(2,1)}) %all-gather.7.cloned.1.call-update) | async-done | bytes 12582928 | tf_op jit(solution)/shard_map/all_gather | solution.py:59
  161.8 17.2 %fusion.50 = f32[8,384,1536]{2,1,0:T(8,128)} fusion(bf16[8,384,512]{2,1,0:T(8,128)(2,1)} %all-gather.5.cloned.1.call-done, bf16[8,512,1536]{1,2,0:T(8,128)(2,1)} %all-gather.7.cloned.1.call-done), kind=kOutput, calls=%fused_computation.66 | convolution fusion | flops 4831838208 | bytes 34603008 | tf_op jit(solution)/shard_map/mrw,mwc->mrc/dot_general | solution.py:65
  179.1 0.0 copy-done.7
  179.1 9.6 %multiply_reduce_fusion = f32[384,1536]{1,0:T(8,128)} fusion(f32[8,384,1536]{2,1,0:T(8,128)} %fusion.50, s32[1,8,24,24]{3,2,1,0:T(8,128)S(1)} %copy-done.7, s32[384]{0:T(512)S(1)} %add_select_fusion.1, s32[1536]{0:T(1024)S(1)} %add_select_fusion), kind=kOutput, calls=%fused_computation.2 | convolution fusion | flops 238929408 | bytes 21259776 | tf_op jit(solution)/shard_map/rt,mts,cs->mrc/dot_general | solution.py:64
  188.7 0.0 all-reduce.2.cloned.1.call-update
  188.7 66.2 %all-reduce.2.cloned.1.call-done = f32[384,1536]{1,0:T(8,128)} async-done(((f32[384,1536]{1,0:T(8,128)}), f32[384,1536]{1,0:T(8,128)}) %all-reduce.2.cloned.1.call-update) | async-done | bytes 2359312 | tf_op jit(solution)/shard_map/psum | solution.py:72
  254.9 3.6 %fusion.49 = (bf16[384,1536]{1,0:T(8,128)(2,1)S(1)}, f32[384,1536]{1,0:T(8,128)}) fusion(f32[384,1536]{1,0:T(8,128)S(1)} %copy-done.3, f32[384,1536]{1,0:T(8,128)} %all-reduce.2.cloned.1.call-done), kind=kLoop, calls=%fused_computation.64 | loop fusion | flops 1179648 | bytes 8257536 | tf_op jit(solution)/shard_map/convert.1
  258.4 1.0 copy-done.5
  259.5 1.3 broadcast_in_dim.33
  260.8 8.0 %all-to-all-start.1 = ((bf16[16,32,1536]{2,1,0:T(8,128)(2,1)}), bf16[16,32,1536]{2,1,0:T(8,128)(2,1)S(1)}, u32[]{:S(2)}, u32[]{:S(2)}) async-start(bf16[16,32,1536]{2,1,0:T(8,128)(2,1)} %broadcast_in_dim.33), calls=%async_computation.1 | async-start | bytes 3145728 | tf_op jit(solution)/shard_map/all_to_all | solution.py:19
  268.8 0.2 all-gather.9.cloned.1.call-start
  269.0 2.1 convolution_convert_fusion.2
  271.1 0.0 all-gather.9.cloned.1.call-update
  271.2 28.6 %all-gather.9.cloned.1.call-done = bf16[1536,512]{1,0:T(8,128)(2,1)} async-done(((bf16[384,512]{1,0:T(8,128)(2,1)}), bf16[1536,512]{1,0:T(8,128)(2,1)}) %all-gather.9.cloned.1.call-update) | async-done | bytes 1572880 | tf_op jit(solution)/shard_map/all_gather | solution.py:27
  299.8 1.0 slice.17
  300.9 0.0 copy-start.4
  300.9 6.4 %all-to-all-done.1 = bf16[16,32,1536]{2,1,0:T(8,128)(2,1)S(1)} async-done(((bf16[16,32,1536]{2,1,0:T(8,128)(2,1)}), bf16[16,32,1536]{2,1,0:T(8,128)(2,1)S(1)}, u32[]{:S(2)}, u32[]{:S(2)}) %all-to-all-start.1) | async-done | bytes 1572896 | tf_op jit(solution)/shard_map/all_to_all | solution.py:19
  307.3 2.9 gather_fusion
  310.2 2.6 convolution_convert_fusion
  312.9 1.1 copy-done.2
  314.0 1.6 copy.18
  315.6 2.2 fusion.51
  317.8 0.0 copy-start.1
  317.8 0.0 copy-done.9
  317.8 3.8 %fusion.2 = f32[384,1536]{1,0:T(8,128)} fusion(f32[384,1536]{1,0:T(8,128)} %get-tuple-element.10, f32[384,1536]{1,0:T(8,128)S(1)} %fusion.51, s32[384]{0:T(512)S(1)} %add_select_fusion.1, s32[1536]{0:T(1024)S(1)} %add_select_fusion, s32[24,24]{1,0:T(8,128)S(1)} %copy-done.9), kind=kOutput, calls=%fused_computation.6 | convolution fusion | flops 29980224 | bytes 7087872 | tf_op jit(solution)/shard_map/rt,ts,cs->rc/dot_general | solution.py:83
  321.6 0.0 copy-done.1
  (22 shorter events, 0.1 us)
Async XLA Ops:
  7.2 1.2 copy-start
  7.2 3.8 %copy-start.6 = (bf16[1,8,32,1536]{3,2,1,0:T(8,128)(2,1)S(1)}, bf16[1,8,32,1536]{3,2,1,0:T(8,128)(2,1)}, u32[]{:S(2)}) copy-start(bf16[1,8,32,1536]{3,2,1,0:T(8,128)(2,1)} %param.13) | copy-start | bytes 2359300
  7.2 81.7 %all-gather.5.cloned.1.call-start = ((), (), s32[]{:S(2)}) async-start(), calls=%async_computation.2 | async-start | bytes 3932160 | tf_op jit(solution)/shard_map/all_gather | solution.py:67
  17.6 15.7 %copy-start.8 = (s32[1,8,512]{2,1,0:T(8,128)S(1)}, s32[1,8,512]{2,1,0:T(8,128)}, u32[]{:S(2)}) copy-start(s32[1,8,512]{2,1,0:T(8,128)} %param.16) | copy-start | bytes 49156
  23.3 32.7 %all-to-all-start = ((bf16[16,2,12288]{2,1,0:T(2,128)(2,1)}), bf16[16,2,12288]{2,1,0:T(2,128)(2,1)S(1)}, u32[]{:S(2)}, u32[]{:S(2)}) async-start(bf16[16,2,12288]{2,1,0:T(2,128)(2,1)} %reshape.121), calls=%async_computation | async-start | bytes 1572864 | tf_op jit(solution)/shard_map/all_to_all | solution.py:54
  33.3 128.5 %all-gather.7.cloned.1.call-start = ((), (), s32[]{:S(2)}) async-start(), calls=%async_computation.3 | async-start | bytes 13369344 | tf_op jit(solution)/shard_map/all_gather | solution.py:59
  88.8 166.1 %all-reduce.2.cloned.1.call-start = ((), (), s32[]{:S(2)}) async-start(), calls=%async_computation.4 | async-start | bytes 4718592 | tf_op jit(solution)/shard_map/psum | solution.py:72
  88.9 90.2 %copy-start.7 = (s32[1,8,24,24]{3,2,1,0:T(8,128)S(1)}, s32[1,8,24,24]{3,2,1,0:T(8,128)}, u32[]{:S(2)}) copy-start(s32[1,8,24,24]{3,2,1,0:T(8,128)} %param.17) | copy-start | bytes 55300
  188.7 66.2 %copy-start.3 = (f32[384,1536]{1,0:T(8,128)S(1)}, f32[384,1536]{1,0:T(8,128)}, u32[]{:S(2)}) copy-start(f32[384,1536]{1,0:T(8,128)} %param.11) | copy-start | bytes 7077892
  258.4 1.0 copy-start.5
  259.5 9.5 %copy-start.11 = (bf16[512,512]{1,0:T(8,128)(2,1)S(1)}, bf16[512,512]{1,0:T(8,128)(2,1)}, u32[]{:S(2)}) copy-start(bf16[512,512]{1,0:T(8,128)(2,1)} %param.18) | copy-start | bytes 1572868
  260.8 10.4 %copy-start.10 = (s32[512]{0:T(512)S(1)}, s32[512]{0:T(512)}, u32[]{:S(2)}) copy-start(s32[512]{0:T(512)} %param.20) | copy-start | bytes 6148
  260.8 46.5 %all-to-all-start.1 = ((bf16[16,32,1536]{2,1,0:T(8,128)(2,1)}), bf16[16,32,1536]{2,1,0:T(8,128)(2,1)S(1)}, u32[]{:S(2)}, u32[]{:S(2)}) async-start(bf16[16,32,1536]{2,1,0:T(8,128)(2,1)} %broadcast_in_dim.33), calls=%async_computation.1 | async-start | bytes 3145728 | tf_op jit(solution)/shard_map/all_to_all | solution.py:19
  268.8 31.1 %all-gather.9.cloned.1.call-start = ((), (), s32[]{:S(2)}) async-start(), calls=%async_computation.5 | async-start | bytes 1966080 | tf_op jit(solution)/shard_map/all_gather | solution.py:27
  300.9 14.7 %copy-start.4 = (bf16[384,512]{1,0:T(8,128)(2,1)}, bf16[384,512]{1,0:T(8,128)(2,1)S(1)}, u32[]{:S(2)}) copy-start(bf16[384,512]{1,0:T(8,128)(2,1)S(1)} %slice.17) | copy-start | bytes 1179652
  307.3 2.9 copy-start.12
  312.9 1.2 copy-start.2
  315.6 2.2 copy-start.9
  317.8 3.8 %copy-start.1 = (bf16[1,2,512,512]{3,2,1,0:T(8,128)(2,1)S(1)}, bf16[1,2,512,512]{3,2,1,0:T(8,128)(2,1)}, u32[]{:S(2)}) copy-start(bf16[1,2,512,512]{3,2,1,0:T(8,128)(2,1)} %param.14) | copy-start | bytes 3145732
Sparse Core Ops, SparseCore 0:
  11.1 45.6 all-gather.4
  88.9 72.8 all-gather.6
  188.8 66.0 all-reduce.1
  271.7 28.1 all-gather.8
where the time goes:
time: 329 us; the launch traced here: 328 us
  waiting for transfers between devices  197 us (60%)
  local copies, waits for them, and re-layouts  50.8 us (15%)
  matrix products  44.6 us (14%)
  starting transfers between devices  18.3 us (6%)
  between operations  14 us (4%)
  other arithmetic  3.63 us (1%)
    all_gather x1, waiting for transfers between devices, shards(): upper_all = lax.all_gather(finished, 'row', axis=2, tiled=True)  72.9 us
    psum x1, waiting for transfers between devices, shards(): total = lax.psum(contrib, 'layer')  66.2 us
    all_gather x1, waiting for transfers between devices, from_root(): lax.all_gather(x, axis)  28.6 us
    all_to_all x1, waiting for transfers between devices, shards(): lax.all_to_all(upper_local, 'row', split_axis=2, concat_axis=1, tiled=True)  22.6 us
    gather x1, local copies, waits for them, and re-layouts, shards(): jnp.take_along_axis(column_share, leaf_pivots[0][:, :, None], axis=1)  21.7 us
    unnamed x32, local copies, waits for them, and re-layouts  19.9 us
    dot_general x1, matrix products, shards(): jnp.einsum('mrw,mwc->mrc', lax.all_gather(own_lower, 'col', axis=0, tiled...  17.2 us
    all_to_all x1, starting transfers between devices, shards(): lax.all_to_all(upper_local, 'row', split_axis=2, concat_axis=1, tiled=True)  9.97 us
  transfers between devices with their start and end apart: 6, of which 5 were waited for; matrix products, arithmetic and copies ran while one was open for 15% of the time, Pallas kernels for 0%

commit v1 on v0

v1 whole, which is shorter than its diff:
```python
import jax
import jax.numpy as jnp
from jax import lax
from jax.experimental import pallas as pl
from jax.experimental.pallas import tpu as pltpu
from jax.sharding import PartitionSpec as P

MESH = pl.DeviceIdType.MESH
F32 = jnp.float32
BF = jnp.bfloat16
W = 512
TB = 256
LEAVES = 8
NL = 4
NR = 16
NX = 4
RB = 384
PB = 32
CB = 1536
CW = 256
NC = CB // CW
OWN = RB // NL
ZS = 7


def kernel(
    anc,
    ll,
    lu,
    lui,
    lli,
    piv,
    tiles,
    aui,
    ali,
    apiv,
    atiles,
    o_low,
    o_up,
    o_sch,
    ubuf,
    mbuf,
    v_ll,
    v_lui,
    v_lli,
    v_aui,
    v_ali,
    v_alip,
    v_piv,
    v_apiv,
    v_anc,
    part,
    pst,
    rrecv,
    asum,
    pvt,
    v_low,
    v_up,
    v_sch,
    s_tiles,
    s_atiles,
    in_sem,
    own_sem,
    z_ss,
    z_rs,
    d_ss,
    d_rs,
    x_ss,
    x_rs,
    r_ss,
    r_rs,
    a_ss,
    a_rs,
    p_ss,
    p_rs,
    q_ss,
    q_rs,
    l_ss,
    l_rs,
    out_sem,
):
    l = lax.axis_index("layer")
    r = lax.axis_index("row")
    x = lax.axis_index("col")

    def row_of(step):
        return lax.rem(r + (2 * step + 2 * NR), NR)

    z_dev = {1: (l, row_of(1), x), -1: (l, row_of(-1), x)}
    partner = (l, r + 1 - 2 * lax.rem(r, 2), x)

    def layer_of(d):
        return lax.rem(l + d, NL)

    def col_of(d):
        return lax.rem(x + d + NX, NX)

    loads = {}

    def load(name, src, dst, index):
        loads[name] = pltpu.make_async_copy(src, dst, in_sem.at[index])
        loads[name].start()

    for c in range(NC):
        cp = pltpu.make_async_copy(
            lu.at[0, :, :, pl.ds(c * CW, CW)],
            ubuf.at[c, :, pl.ds(pl.multiple_of(r * PB, PB), PB), :],
            own_sem.at[c],
        )
        cp.start()
        loads[("own", c)] = cp
    load("ll", ll.at[0], v_ll, 0)
    load("lui", lui.at[0], v_lui, 1)
    load("lli", lli.at[0, pl.ds(2 * x, 2)], v_lli, 2)
    load("piv", piv.at[0], v_piv, 3)
    load("tiles", tiles.at[0], s_tiles, 4)
    load("aui", aui, v_aui, 5)
    load("ali", ali, v_ali, 6)
    load("apiv", apiv, v_apiv, 7)
    load("atiles", atiles, s_atiles, 8)
    load("anc", anc.at[pl.ds(pl.multiple_of(l * OWN, OWN), OWN), :], v_anc, 9)

    barrier = pltpu.get_barrier_semaphore()
    others = [z_dev[1], z_dev[-1], partner]
    others += [(layer_of(d), r, x) for d in (1, 2, 3)]
    others += [(l, r, col_of(d)) for d in (1, 2, 3)]
    for dev in others:
        pl.semaphore_signal(barrier, inc=1, device_id=dev, device_id_type=MESH)
    pl.semaphore_wait(barrier, len(others))

    sent = []

    def send(src, dst, ss, rs, dev):
        cp = pltpu.make_async_remote_copy(
            src_ref=src, dst_ref=dst, send_sem=ss, recv_sem=rs, device_id=dev, device_id_type=MESH
        )
        cp.start()
        sent.append(cp)
        return cp

    zc = {}
    dc = {}

    def block(b):
        return pl.ds(pl.multiple_of(b * PB, PB), PB)

    def z_half(s, dr):
        return s % 2 if dr > 0 else 1 - s % 2

    def z_send(c, s):
        for dr in (1, -1):
            i = 0 if dr > 0 else 1
            if s >= 2:
                zc[c, dr, s - 2].wait_recv()
            h = z_half(s, dr)
            b = row_of(-dr * (s // 2))
            dst = ubuf.at[c, pl.ds(4 * h, 4), block(b), :]
            src = lu.at[0, pl.ds(4 * h, 4), :, pl.ds(c * CW, CW)] if s < 2 else dst
            zc[c, dr, s] = send(src, dst, z_ss.at[c, i, s], z_rs.at[c, i, s], z_dev[dr])
        if s == 0:
            d_send(c, 0, 0)
        if s in (3, 5):
            d_send(c, s // 2, 1)
            d_send(c, s // 2, -1)

    def d_send(c, hop, dr):
        i = 0 if hop == 0 else (7 if hop == 4 else 2 * hop - 1 + (dr < 0))
        b = row_of(-dr * hop)
        dst = ubuf.at[c, :, block(b), :]
        src = lu.at[0, :, :, pl.ds(c * CW, CW)] if hop == 0 else dst
        dc[c, i] = send(src, dst, d_ss.at[c, i], d_rs.at[c, i], partner)

    def z_last(c, s):
        for dr in (1, -1):
            zc[c, dr, s].wait_recv()
        if s == 5:
            d_send(c, 3, 1)
            d_send(c, 3, -1)
        else:
            d_send(c, 4, 1)

    xc = {}

    def onehot_rows(row_vector):
        rows = lax.broadcasted_iota(jnp.int32, (W, W), 0)
        return jnp.where(rows == row_vector, 1.0, 0.0).astype(BF)

    def times_t(a, b):
        return lax.dot_general(a, b, (((1,), (1,)), ((), ())), preferred_element_type=F32)

    def left_factor(j):
        if j == 0:
            for name in ("ll", "lui", "lli", "piv"):
                loads[name].wait()
        k = 2 * x + j
        lower = jnp.dot(v_ll[j], v_lui[j], preferred_element_type=F32).astype(BF)
        both = jnp.dot(lower, v_lli[j], preferred_element_type=F32).astype(BF)
        mbuf[k] = times_t(both, onehot_rows(v_piv[pl.ds(k, 1), :])).astype(BF)
        if j == 1:
            x_send(-1, 0, k)
            x_send(-1, 1, k - 1)
        x_send(1, j, k)

    def x_send(dr, slot, k):
        i = 0 if dr > 0 else 1
        ref = mbuf.at[k]
        xc[dr, slot] = send(ref, ref, x_ss.at[i, slot], x_rs.at[i, slot], (l, r, col_of(dr)))

    def x_relay():
        xc[1, 0].wait_recv()
        x_send(1, 2, 2 * col_of(-1))
        xc[-1, 0].wait_recv()
        x_send(-1, 2, 2 * col_of(1) + 1)

    def x_done():
        for dr in (1, -1):
            for slot in (1, 2):
                xc[dr, slot].wait_recv()

    def anc_left():
        loads["ali"].wait()
        loads["apiv"].wait()
        v_alip[...] = times_t(v_ali[...], onehot_rows(v_apiv[...])).astype(BF)

    def ready(c):
        for i in range(8):
            dc[c, i].wait_recv()
        loads["own", c].wait()

    def products(c, first, count):
        def one(k, carry):
            prod = jnp.dot(mbuf[k], ubuf[c, k], preferred_element_type=F32)
            for p in range(3):
                tile = s_tiles[k, (3 * r + p) // 2, NC * x + c].astype(F32)
                rows = slice(128 * p, 128 * p + 128)
                part[c, rows, :] = part[c, rows, :] + tile * prod[rows, :]
            return carry

        if first == 0:
            part[c] = jnp.zeros((RB, CW), F32)
        lax.fori_loop(first, first + count, one, 0)

    rc = {}
    ac = {}

    def own_rows(layer):
        return pl.ds(pl.multiple_of(layer * OWN, OWN), OWN)

    def scatter(c):
        pst[c] = part[c].astype(BF)
        for d in (2, 1, 3):
            to = layer_of(d)
            rc[c, d] = send(
                pst.at[c, own_rows(to), :], rrecv.at[c, d - 1], r_ss.at[c, d - 1], r_rs.at[c, d - 1], (to, r, x)
            )

    def add_up(c):
        if c == 0:
            loads["anc"].wait()
        for d in (1, 2, 3):
            rc[c, d].wait_recv()
        total = part[c, own_rows(l), :] + v_anc[:, c * CW : c * CW + CW]
        for d in range(3):
            total = total + rrecv[c, d].astype(F32)
        asum[c, own_rows(l), :] = total.astype(BF)
        ref = asum.at[c, own_rows(l), :]
        for d in (2, 1, 3):
            ac[c, d] = send(ref, ref, a_ss.at[c, d - 1], a_rs.at[c, d - 1], (layer_of(d), r, x))

    pc = {}
    qc = {}

    def p_send(c, hop, dr):
        i = 0 if dr > 0 else 1
        b = row_of(-dr * hop)
        dst = pvt.at[c, block(b), :]
        src = asum.at[c, pl.ds(0, PB), :] if hop == 0 else dst
        pc[c, dr, hop] = send(src, dst, p_ss.at[c, i, hop], p_rs.at[c, i, hop], z_dev[dr])

    def q_send(c, hop, dr):
        i = 0 if hop == 0 else 2 * hop - 1 + (dr < 0)
        b = row_of(-dr * hop)
        dst = pvt.at[c, block(b), :]
        src = asum.at[c, pl.ds(0, PB), :] if hop == 0 else dst
        qc[c, i] = send(src, dst, q_ss.at[c, i], q_rs.at[c, i], partner)

    def pivots(c, hop):
        if hop == 0:
            for d in (1, 2, 3):
                ac[c, d].wait_recv()
            p_send(c, 0, 1)
            p_send(c, 0, -1)
            q_send(c, 0, 0)
            pvt[c, block(r), :] = asum[c, 0:PB, :]
            return
        for dr in (1, -1):
            if hop == 4 and dr < 0:
                continue
            pc[c, dr, hop - 1].wait_recv()
            if hop < 3 or (hop == 3 and dr > 0):
                p_send(c, hop, dr)
            q_send(c, hop, dr)

    def anc_low():
        loads["aui"].wait()

        @pl.when(x == 0)
        def _():
            low = jnp.dot(asum[0], v_aui[0:CW, :], preferred_element_type=F32)
            low = low + jnp.dot(asum[1], v_aui[CW : 2 * CW, :], preferred_element_type=F32)
            v_low[...] = low.astype(BF)
            for d in (2, 1, 3):
                low_copy(d).start()

    def low_copy(d):
        return pltpu.make_async_remote_copy(
            src_ref=v_low,
            dst_ref=v_low,
            send_sem=l_ss.at[d - 1],
            recv_sem=l_rs,
            device_id=(l, r, col_of(d)),
            device_id_type=MESH,
        )

    def low_done():
        @pl.when(x != 0)
        def _():
            low_copy(1).wait_recv()

        @pl.when(x == 0)
        def _():
            for d in (1, 2, 3):
                low_copy(d).wait_send()

        put(v_low, o_low)

    outs = []

    def put(src, dst):
        cp = pltpu.make_async_copy(src, dst, out_sem.at[len(outs)])
        cp.start()
        outs.append(cp)

    def finish(c):
        for i in range(8):
            qc[c, i].wait_recv()
        v_up[c] = jnp.dot(v_alip[...], pvt[c], preferred_element_type=F32).astype(BF)
        put(v_up.at[c], o_up.at[:, pl.ds(c * CW, CW)])
        prod = jnp.dot(v_low[...], v_up[c], preferred_element_type=F32)
        for p in range(3):
            tile = s_atiles[(3 * r + p) // 2, NC * x + c].astype(F32)
            rows = slice(128 * p, 128 * p + 128)
            v_sch[c, rows, :] = asum[c, rows, :].astype(F32) - tile * prod[rows, :]
        put(v_sch.at[c], o_sch.at[:, pl.ds(c * CW, CW)])

    def comp(c, part_index):
        if part_index == 0:
            ready(c)
            products(c, 0, 4)
        else:
            products(c, 4, 4)
            scatter(c)

    def m_ready():
        x_done()
        loads["tiles"].wait()

    events = {}

    def at(g, fn, *args):
        events.setdefault(g, []).append((fn, args))

    at(1, left_factor, 0)
    at(2, left_factor, 1)
    at(5, anc_left)
    at(10, x_relay)
    at(20, m_ready)
    for c, g in ((0, 20), (1, 22), (2, 24), (3, 30), (4, 37)):
        at(g, comp, c, 0)
        at(g + 1, comp, c, 1)
    for c, g in ((0, 25), (1, 27), (2, 29), (3, 35), (4, 41)):
        at(g, add_up, c)
    for c, g in ((0, 29), (1, 31), (2, 33), (3, 37)):
        for hop in range(5):
            at(g + hop, pivots, c, hop)
    at(31, anc_low)

    for c in range(NC):
        for s in range(ZS):
            z_send(c, s)
            if c > 0 and s < 2:
                z_last(c - 1, 5 + s)
            for fn, args in events.get(ZS * c + s, []):
                fn(*args)
    loads["atiles"].wait()
    c = NC - 1
    z_last(c, 5)
    z_last(c, 6)
    comp(c, 0)
    comp(c, 1)
    pivots(c - 1, 0)
    low_done()
    finish(0)
    pivots(c - 1, 1)
    finish(1)
    pivots(c - 1, 2)
    add_up(c)
    pivots(c - 1, 3)
    finish(2)
    pivots(c - 1, 4)
    pivots(c, 0)
    finish(3)
    for hop in range(1, 5):
        pivots(c, hop)
        if hop == 1:
            finish(4)
    finish(c)
    for cp in sent:
        cp.wait_send()
    for cp in outs:
        cp.wait()


def shards(*args):
    any_space = pl.BlockSpec(memory_space=pl.ANY)
    dma = pltpu.SemaphoreType.DMA
    vmem = pltpu.VMEM
    return pl.pallas_call(
        kernel,
        out_shape=(
            jax.ShapeDtypeStruct((RB, W), BF),
            jax.ShapeDtypeStruct((W, CB), BF),
            jax.ShapeDtypeStruct((RB, CB), F32),
        ),
        in_specs=[any_space] * 11,
        out_specs=(any_space,) * 3,
        scratch_shapes=[
            vmem((NC, LEAVES, W, CW), BF),
            vmem((LEAVES, RB, W), BF),
            vmem((2, RB, W), BF),
            vmem((2, W, W), BF),
            vmem((2, W, W), BF),
            vmem((W, W), BF),
            vmem((W, W), BF),
            vmem((W, W), BF),
            vmem((LEAVES, W), jnp.int32),
            vmem((1, W), jnp.int32),
            vmem((OWN, CB), F32),
            vmem((NC, RB, CW), F32),
            vmem((NC, RB, CW), BF),
            vmem((NC, 3, OWN, CW), BF),
            vmem((NC, RB, CW), BF),
            vmem((NC, W, CW), BF),
            vmem((RB, W), BF),
            vmem((NC, W, CW), BF),
            vmem((NC, RB, CW), F32),
            pltpu.SMEM((LEAVES, 24, 24), jnp.int32),
            pltpu.SMEM((24, 24), jnp.int32),
            dma((10,)),
            dma((NC,)),
            dma((NC, 2, ZS)),
            dma((NC, 2, ZS)),
            dma((NC, 8)),
            dma((NC, 8)),
            dma((2, 3)),
            dma((2, 3)),
            dma((NC, 3)),
            dma((NC, 3)),
            dma((NC, 3)),
            dma((NC, 3)),
            dma((NC, 2, 4)),
            dma((NC, 2, 4)),
            dma((NC, 8)),
            dma((NC, 8)),
            dma((3,)),
            dma(()),
            dma((2 * NC + 1,)),
        ],
        compiler_params=pltpu.CompilerParams(
            collective_id=0, has_side_effects=True, vmem_limit_bytes=56 * 2**20
        ),
    )(*args[:9], args[9].reshape(1, W), args[10])


def solution(mesh):
    return jax.shard_map(
        shards,
        mesh=mesh,
        in_specs=(
            P("row", "col"),
            P("layer", "col", "row", None),
            P("layer", None, "row", "col"),
            P("layer", "col", None, None),
            P("layer", None, None, None),
            P("layer", None, None),
            P("layer", None, None, None),
            P(),
            P(),
            P(),
            P(),
        ),
        out_specs=(P("row", None), P(None, "col"), P("row", "col")),
        check_vma=False,
    )
```

time: 329 us -> 142 us (0.43)
  waiting for transfers between devices: 197 us -> 0 us
  Pallas kernels: 0 us -> 135 us
  local copies, waits for them, and re-layouts: 50.8 us -> 5.98 us
  matrix products: 44.6 us -> 0 us
  starting transfers between devices: 18.3 us -> 0 us
  between operations: 14 us -> 0.65 us
  other arithmetic: 3.63 us -> 0 us
    pallas_call x0 -> x1, Pallas kernels: none -> 135 us  [shards(): pl.pallas_call(kernel, out_shape=(jax.ShapeDtypeStruct((RB, W), BF), jax....]
    all_gather x3 -> x0, waiting for transfers between devices: 102 us -> none  [the longest x1 72.9 us: shards(): upper_all = lax.all_gather(finished, 'row', axis=2, tiled=True)]
    psum x1 -> x0, waiting for transfers between devices: 66.2 us -> none  [shards(): total = lax.psum(contrib, 'layer')]
    dot_general x8 -> x0, matrix products: 44.6 us -> none  [the longest x1 17.2 us: shards(): jnp.einsum('mrw,mwc->mrc', lax.all_gather(own_lower, 'col', axis=0, tiled...]
    all_to_all x2 -> x0, waiting for transfers between devices: 29 us -> none  [the longest x1 22.6 us: shards(): lax.all_to_all(upper_local, 'row', split_axis=2, concat_axis=1, tiled=True)]
    gather x2 -> x0, local copies, waits for them, and re-layouts: 24.6 us -> none  [the longest x1 21.7 us: shards(): jnp.take_along_axis(column_share, leaf_pivots[0][:, :, None], axis=1)]
    all_to_all x2 -> x0, starting transfers between devices: 18 us -> none  [the longest x1 9.97 us: shards(): lax.all_to_all(upper_local, 'row', split_axis=2, concat_axis=1, tiled=True)]
    unnamed x32 -> x5, local copies, waits for them, and re-layouts: 19.9 us -> 5.98 us
  transfers between devices with their start and end apart: 6 -> 0, of which waited for: 5 -> 0; matrix products, arithmetic and copies ran while one was open for 15% -> 0% of each run, Pallas kernels for 0% -> 0%
where the time goes in v1:
time: 142 us
  Pallas kernels  135 us (95%)
  local copies, waits for them, and re-layouts  5.98 us (4%)
    pallas_call x1, Pallas kernels, shards(): pl.pallas_call(kernel, out_shape=(jax.ShapeDtypeStruct((RB, W), BF), jax....  135 us
    unnamed x5, local copies, waits for them, and re-layouts  5.98 us

profile of v1, /device:TPU:1, one launch (start us, length us, event | category | flops | bytes accessed | tf_op | source)
XLA Modules:
  0.0 141.8 jit_solution(9089531158284852917)
XLA Ops:
  0.6 135.2 %shard_map.130 = (bf16[384,512]{1,0:T(8,128)(2,1)}, bf16[512,1536]{1,0:T(8,128)(2,1)}, f32[384,1536]{1,0:T(8,128)}) custom-call(f32[384,1536]{1,0:T(8,128)} %anc.1, bf16[1,2,384,512]{3,2,1,0:T(8,128)(2,1)} %ll.1, bf16[1,8,32,1536]{3,2,1,0:T(8,128)(2,1)} %lu.1, bf16[1,2,512,512]{3,2,1,0:T(8,128)(2,1)} %lui.1, bf16[1,8,512,512]{3,2,1,0:T(8,128)(2,1)} %lli.1, ...), custom_call_target="tpu_custom_call" | custom-call | tf_op jit(solution)/shard_map/pallas_call | solution.py:428
  135.8 0.0 copy-start
  135.8 1.9 %copy.17 = bf16[384,512]{1,0:T(8,128)(2,1)} copy(bf16[384,512]{1,0:T(8,128)(2,1)} %get-tuple-element.6) | data formatting | bytes 786432
  137.7 2.7 %copy.18 = bf16[512,1536]{1,0:T(8,128)(2,1)} copy(bf16[512,1536]{1,0:T(8,128)(2,1)} %get-tuple-element.7) | data formatting | bytes 3145728
  140.4 0.0 copy-done
  140.4 1.4 copy.19
Async XLA Ops:
  135.8 4.6 %copy-start = (f32[384,1536]{1,0:T(8,128)S(1)}, f32[384,1536]{1,0:T(8,128)}, u32[]{:S(2)}) copy-start(f32[384,1536]{1,0:T(8,128)} %get-tuple-element.8) | copy-start | bytes 7077892

commit v2 on v1

--- a/solution.py
+++ b/solution.py
@@ -20,7 +20,23 @@
 CW = 256
 NC = CB // CW
 OWN = RB // NL
-ZS = 7
+GAP = 4
+
+
+def ring_order():
+    left = [(c, h, i) for c in range(NC) for h in range(4) for i in range(2) if h < 3 or i == 0]
+    order, place = [], {}
+    while left:
+        g = len(order)
+        fit = [m for m in left if m[1] == 0 or place.get((m[0], m[1] - 1, m[2]), g) + GAP <= g]
+        order.append(fit[0] if fit else None)
+        if fit:
+            place[fit[0]] = g
+            left.remove(fit[0])
+    return order, place
+
+
+ORDER, PLACE = ring_order()
 
 
 def kernel(
@@ -35,9 +51,9 @@
     ali,
     apiv,
     atiles,
-    o_low,
-    o_up,
-    o_sch,
+    v_low,
+    v_up,
+    v_sch,
     ubuf,
     mbuf,
     v_ll,
@@ -54,9 +70,8 @@
     rrecv,
     asum,
     pvt,
-    v_low,
-    v_up,
-    v_sch,
+    v_top,
+    precv,
     s_tiles,
     s_atiles,
     in_sem,
@@ -77,7 +92,8 @@
     q_rs,
     l_ss,
     l_rs,
-    out_sem,
+    v_ss,
+    v_rs,
 ):
     l = lax.axis_index("layer")
     r = lax.axis_index("row")
@@ -118,6 +134,7 @@
     load("ali", ali, v_ali, 6)
     load("apiv", apiv, v_apiv, 7)
     load("atiles", atiles, s_atiles, 8)
+    load("top", anc.at[pl.ds(0, PB), :], v_top, 10)
     load("anc", anc.at[pl.ds(pl.multiple_of(l * OWN, OWN), OWN), :], v_anc, 9)
 
     barrier = pltpu.get_barrier_semaphore()
@@ -144,24 +161,21 @@
     def block(b):
         return pl.ds(pl.multiple_of(b * PB, PB), PB)
 
-    def z_half(s, dr):
-        return s % 2 if dr > 0 else 1 - s % 2
-
-    def z_send(c, s):
+    def z_send(c, hop, i):
         for dr in (1, -1):
-            i = 0 if dr > 0 else 1
-            if s >= 2:
-                zc[c, dr, s - 2].wait_recv()
-            h = z_half(s, dr)
-            b = row_of(-dr * (s // 2))
-            dst = ubuf.at[c, pl.ds(4 * h, 4), block(b), :]
-            src = lu.at[0, pl.ds(4 * h, 4), :, pl.ds(c * CW, CW)] if s < 2 else dst
-            zc[c, dr, s] = send(src, dst, z_ss.at[c, i, s], z_rs.at[c, i, s], z_dev[dr])
-        if s == 0:
+            n = 0 if dr > 0 else 1
+            if hop:
+                zc[c, dr, hop - 1, i].wait_recv()
+            h = i if dr > 0 else 1 - i
+            dst = ubuf.at[c, pl.ds(4 * h, 4), block(row_of(-dr * hop)), :]
+            src = lu.at[0, pl.ds(4 * h, 4), :, pl.ds(c * CW, CW)] if hop == 0 else dst
+            slot = 2 * hop + i
+            zc[c, dr, hop, i] = send(src, dst, z_ss.at[c, n, slot], z_rs.at[c, n, slot], z_dev[dr])
+        if hop == 0 and i == 0:
             d_send(c, 0, 0)
-        if s in (3, 5):
-            d_send(c, s // 2, 1)
-            d_send(c, s // 2, -1)
+        if hop in (1, 2) and i == 1:
+            d_send(c, hop, 1)
+            d_send(c, hop, -1)
 
     def d_send(c, hop, dr):
         i = 0 if hop == 0 else (7 if hop == 4 else 2 * hop - 1 + (dr < 0))
@@ -170,10 +184,10 @@
         src = lu.at[0, :, :, pl.ds(c * CW, CW)] if hop == 0 else dst
         dc[c, i] = send(src, dst, d_ss.at[c, i], d_rs.at[c, i], partner)
 
-    def z_last(c, s):
+    def z_last(c, hop):
         for dr in (1, -1):
-            zc[c, dr, s].wait_recv()
-        if s == 5:
+            zc[c, dr, hop, 1 if hop == 2 else 0].wait_recv()
+        if hop == 2:
             d_send(c, 3, 1)
             d_send(c, 3, -1)
         else:
@@ -227,18 +241,15 @@
             dc[c, i].wait_recv()
         loads["own", c].wait()
 
-    def products(c, first, count):
-        def one(k, carry):
-            prod = jnp.dot(mbuf[k], ubuf[c, k], preferred_element_type=F32)
-            for p in range(3):
-                tile = s_tiles[k, (3 * r + p) // 2, NC * x + c].astype(F32)
-                rows = slice(128 * p, 128 * p + 128)
-                part[c, rows, :] = part[c, rows, :] + tile * prod[rows, :]
-            return carry
-
-        if first == 0:
-            part[c] = jnp.zeros((RB, CW), F32)
-        lax.fori_loop(first, first + count, one, 0)
+    def products(c, p):
+        rows = slice(128 * p, 128 * p + 128)
+        total = None
+        for k in range(LEAVES):
+            tile = s_tiles[k, (3 * r + p) // 2, NC * x + c].astype(F32)
+            prod = tile * jnp.dot(mbuf[k, rows, :], ubuf[c, k], preferred_element_type=F32)
+            total = prod if total is None else total + prod
+        part[c, rows, :] = total
+        pst[c, rows, :] = total.astype(BF)
 
     rc = {}
     ac = {}
@@ -247,7 +258,6 @@
         return pl.ds(pl.multiple_of(layer * OWN, OWN), OWN)
 
     def scatter(c):
-        pst[c] = part[c].astype(BF)
         for d in (2, 1, 3):
             to = layer_of(d)
             rc[c, d] = send(
@@ -267,31 +277,51 @@
         for d in (2, 1, 3):
             ac[c, d] = send(ref, ref, a_ss.at[c, d - 1], a_rs.at[c, d - 1], (layer_of(d), r, x))
 
+    def gathered(c):
+        if c not in done:
+            done.add(c)
+            for d in (1, 2, 3):
+                ac[c, d].wait_recv()
+
+    done = set()
+
     pc = {}
     qc = {}
 
     def p_send(c, hop, dr):
         i = 0 if dr > 0 else 1
         b = row_of(-dr * hop)
-        dst = pvt.at[c, block(b), :]
-        src = asum.at[c, pl.ds(0, PB), :] if hop == 0 else dst
-        pc[c, dr, hop] = send(src, dst, p_ss.at[c, i, hop], p_rs.at[c, i, hop], z_dev[dr])
+        ref = pvt.at[c, block(b), :]
+        pc[c, dr, hop] = send(ref, ref, p_ss.at[c, i, hop], p_rs.at[c, i, hop], z_dev[dr])
 
     def q_send(c, hop, dr):
         i = 0 if hop == 0 else 2 * hop - 1 + (dr < 0)
         b = row_of(-dr * hop)
-        dst = pvt.at[c, block(b), :]
-        src = asum.at[c, pl.ds(0, PB), :] if hop == 0 else dst
-        qc[c, i] = send(src, dst, q_ss.at[c, i], q_rs.at[c, i], partner)
+        ref = pvt.at[c, block(b), :]
+        qc[c, i] = send(ref, ref, q_ss.at[c, i], q_rs.at[c, i], partner)
+
+    vc = {}
+
+    def spread(c):
+        precv[c, l] = pst[c, 0:PB, :]
+        for d in (2, 1, 3):
+            vc[c, d] = send(
+                pst.at[c, pl.ds(0, PB), :], precv.at[c, l], v_ss.at[c, d - 1], v_rs.at[c, d - 1], (layer_of(d), r, x)
+            )
 
     def pivots(c, hop):
         if hop == 0:
+            if c == 0:
+                loads["top"].wait()
             for d in (1, 2, 3):
-                ac[c, d].wait_recv()
+                vc[c, d].wait_recv()
+            total = v_top[:, c * CW : c * CW + CW]
+            for d in range(NL):
+                total = total + precv[c, d].astype(F32)
+            pvt[c, block(r), :] = total.astype(BF)
             p_send(c, 0, 1)
             p_send(c, 0, -1)
             q_send(c, 0, 0)
-            pvt[c, block(r), :] = asum[c, 0:PB, :]
             return
         for dr in (1, -1):
             if hop == 4 and dr < 0:
@@ -303,6 +333,8 @@
 
     def anc_low():
         loads["aui"].wait()
+        gathered(0)
+        gathered(1)
 
         @pl.when(x == 0)
         def _():
@@ -332,34 +364,24 @@
             for d in (1, 2, 3):
                 low_copy(d).wait_send()
 
-        put(v_low, o_low)
-
-    outs = []
-
-    def put(src, dst):
-        cp = pltpu.make_async_copy(src, dst, out_sem.at[len(outs)])
-        cp.start()
-        outs.append(cp)
-
     def finish(c):
         for i in range(8):
             qc[c, i].wait_recv()
+        gathered(c)
         v_up[c] = jnp.dot(v_alip[...], pvt[c], preferred_element_type=F32).astype(BF)
-        put(v_up.at[c], o_up.at[:, pl.ds(c * CW, CW)])
         prod = jnp.dot(v_low[...], v_up[c], preferred_element_type=F32)
         for p in range(3):
             tile = s_atiles[(3 * r + p) // 2, NC * x + c].astype(F32)
             rows = slice(128 * p, 128 * p + 128)
             v_sch[c, rows, :] = asum[c, rows, :].astype(F32) - tile * prod[rows, :]
-        put(v_sch.at[c], o_sch.at[:, pl.ds(c * CW, CW)])
-
-    def comp(c, part_index):
-        if part_index == 0:
-            ready(c)
-            products(c, 0, 4)
-        else:
-            products(c, 4, 4)
-            scatter(c)
+
+    def comp(c):
+        ready(c)
+        products(c, 0)
+        spread(c)
+        products(c, 1)
+        products(c, 2)
+        scatter(c)
 
     def m_ready():
         x_done()
@@ -375,49 +397,75 @@
     at(5, anc_left)
     at(10, x_relay)
     at(20, m_ready)
-    for c, g in ((0, 20), (1, 22), (2, 24), (3, 30), (4, 37)):
-        at(g, comp, c, 0)
-        at(g + 1, comp, c, 1)
-    for c, g in ((0, 25), (1, 27), (2, 29), (3, 35), (4, 41)):
+    for c in range(NC):
+        at(PLACE[c, 2, 1] + GAP, z_last, c, 2)
+        at(PLACE[c, 3, 0] + GAP, z_last, c, 3)
+    for c, g in ((0, 20), (1, 22), (2, 30), (3, 33)):
+        at(g, comp, c)
+    for c, g in ((0, 25), (1, 27), (2, 34), (3, 37)):
+        at(g, pivots, c, 0)
         at(g, add_up, c)
-    for c, g in ((0, 29), (1, 31), (2, 33), (3, 37)):
-        for hop in range(5):
-            at(g + hop, pivots, c, hop)
+    for c, hop, g in ((0, 1, 32), (1, 1, 33), (0, 2, 38), (1, 2, 39)):
+        at(g, pivots, c, hop)
     at(31, anc_low)
 
-    for c in range(NC):
-        for s in range(ZS):
-            z_send(c, s)
-            if c > 0 and s < 2:
-                z_last(c - 1, 5 + s)
-            for fn, args in events.get(ZS * c + s, []):
-                fn(*args)
-    loads["atiles"].wait()
-    c = NC - 1
-    z_last(c, 5)
-    z_last(c, 6)
-    comp(c, 0)
-    comp(c, 1)
-    pivots(c - 1, 0)
+    n = len(ORDER)
+    for g in range(n):
+        if ORDER[g] is not None:
+            z_send(*ORDER[g])
+        for fn, args in events.pop(g, []):
+            fn(*args)
+    for g in sorted(events):
+        for fn, args in events[g]:
+            fn(*args)
+            if fn is z_last and args == (4, 3):
+                comp(4)
+                loads["atiles"].wait()
+    pivots(0, 3)
+    pivots(1, 3)
+    pivots(2, 1)
+    pivots(3, 1)
+    pivots(4, 0)
+    comp(5)
+    add_up(4)
+    pivots(0, 4)
+    pivots(1, 4)
     low_done()
     finish(0)
-    pivots(c - 1, 1)
+    pivots(2, 2)
+    pivots(3, 2)
+    pivots(5, 0)
+    pivots(4, 1)
+    add_up(5)
     finish(1)
-    pivots(c - 1, 2)
-    add_up(c)
-    pivots(c - 1, 3)
+    pivots(2, 3)
+    pivots(3, 3)
+    pivots(5, 1)
+    pivots(4, 2)
+    pivots(2, 4)
+    pivots(3, 4)
     finish(2)
-    pivots(c - 1, 4)
-    pivots(c, 0)
+    pivots(5, 2)
+    pivots(4, 3)
     finish(3)
-    for hop in range(1, 5):
-        pivots(c, hop)
-        if hop == 1:
-            finish(4)
-    finish(c)
+    pivots(4, 4)
+    pivots(5, 3)
+    finish(4)
+    pivots(5, 4)
+    finish(5)
     for cp in sent:
         cp.wait_send()
-    for cp in outs:
+
+
+def write_out(v_low, v_up, v_sch, o_low, o_up, o_sch, sem):
+    copies = [pltpu.make_async_copy(v_low, o_low, sem.at[2 * NC])]
+    for c in range(NC):
+        cols = pl.ds(c * CW, CW)
+        copies.append(pltpu.make_async_copy(v_sch.at[c], o_sch.at[:, cols], sem.at[c]))
+        copies.append(pltpu.make_async_copy(v_up.at[c], o_up.at[:, cols], sem.at[NC + c]))
+    for cp in copies:
+        cp.start()
+    for cp in copies:
         cp.wait()
 
 
@@ -425,15 +473,11 @@
     any_space = pl.BlockSpec(memory_space=pl.ANY)
     dma = pltpu.SemaphoreType.DMA
     vmem = pltpu.VMEM
-    return pl.pallas_call(
+    made = pl.pallas_call(
         kernel,
-        out_shape=(
-            jax.ShapeDtypeStruct((RB, W), BF),
-            jax.ShapeDtypeStruct((W, CB), BF),
-            jax.ShapeDtypeStruct((RB, CB), F32),
-        ),
+        out_shape=(vmem((RB, W), BF), vmem((NC, W, CW), BF), vmem((NC, RB, CW), F32)),
         in_specs=[any_space] * 11,
-        out_specs=(any_space,) * 3,
+        out_specs=(pl.BlockSpec(memory_space=vmem),) * 3,
         scratch_shapes=[
             vmem((NC, LEAVES, W, CW), BF),
             vmem((LEAVES, RB, W), BF),
@@ -451,15 +495,14 @@
             vmem((NC, 3, OWN, CW), BF),
             vmem((NC, RB, CW), BF),
             vmem((NC, W, CW), BF),
-            vmem((RB, W), BF),
-            vmem((NC, W, CW), BF),
-            vmem((NC, RB, CW), F32),
+            vmem((PB, CB), F32),
+            vmem((NC, NL, PB, CW), BF),
             pltpu.SMEM((LEAVES, 24, 24), jnp.int32),
             pltpu.SMEM((24, 24), jnp.int32),
-            dma((10,)),
+            dma((11,)),
             dma((NC,)),
-            dma((NC, 2, ZS)),
-            dma((NC, 2, ZS)),
+            dma((NC, 2, 7)),
+            dma((NC, 2, 7)),
             dma((NC, 8)),
             dma((NC, 8)),
             dma((2, 3)),
@@ -474,12 +517,25 @@
             dma((NC, 8)),
             dma((3,)),
             dma(()),
-            dma((2 * NC + 1,)),
+            dma((NC, 3)),
+            dma((NC, 3)),
         ],
         compiler_params=pltpu.CompilerParams(
             collective_id=0, has_side_effects=True, vmem_limit_bytes=56 * 2**20
         ),
     )(*args[:9], args[9].reshape(1, W), args[10])
+    return pl.pallas_call(
+        write_out,
+        out_shape=(
+            jax.ShapeDtypeStruct((RB, W), BF),
+            jax.ShapeDtypeStruct((W, CB), BF),
+            jax.ShapeDtypeStruct((RB, CB), F32),
+        ),
+        in_specs=[any_space] * 3,
+        out_specs=(any_space,) * 3,
+        scratch_shapes=[dma((2 * NC + 1,))],
+        compiler_params=pltpu.CompilerParams(vmem_limit_bytes=2**20),
+    )(*made)
 
 
 def solution(mesh):

time: 142 us -> 104 us (0.73)
  Pallas kernels: 135 us -> 103 us
  local copies, waits for them, and re-layouts: 5.98 us -> 0 us
    pallas_call x1 -> x2, Pallas kernels: 135 us -> 103 us  [the longest x1 101 us: shards(): pl.pallas_call(kernel, out_shape=(vmem((RB, W), BF), vmem((NC, W, CW), BF...]
    unnamed x5 -> x0, local copies, waits for them, and re-layouts: 5.98 us -> none
where the time goes in v2:
time: 104 us
  Pallas kernels  103 us (99%)
    pallas_call x1, Pallas kernels, shards(): pl.pallas_call(kernel, out_shape=(vmem((RB, W), BF), vmem((NC, W, CW), BF...  101 us
    pallas_call x1, Pallas kernels, shards(): pl.pallas_call(write_out, out_shape=(jax.ShapeDtypeStruct((RB, W), BF), j...  2.15 us

profile of v2, /device:TPU:1, one launch (start us, length us, event | category | flops | bytes accessed | tf_op | source)
XLA Modules:
  0.0 103.6 jit_solution(10272407777083326457)
XLA Ops:
  0.6 100.6 %shard_map.130 = (bf16[384,512]{1,0:T(8,128)(2,1)S(1)}, bf16[6,512,256]{2,1,0:T(8,128)(2,1)S(1)}, f32[6,384,256]{2,1,0:T(8,128)S(1)}) custom-call(f32[384,1536]{1,0:T(8,128)} %anc.1, bf16[1,2,384,512]{3,2,1,0:T(8,128)(2,1)} %ll.1, bf16[1,8,32,1536]{3,2,1,0:T(8,128)(2,1)} %lu.1, bf16[1,2,512,512]{3,2,1,0:T(8,128)(2,1)} %lui.1, bf16[1,8,512,512]{3,2,1,0:T(8,128)(2,1)} %lli.1, ...), custom_call_target="tpu_custom_call" | custom-call | tf_op jit(solution)/shard_map/pallas_call | solution.py:476
  101.3 2.2 %shard_map.131 = (bf16[384,512]{1,0:T(8,128)(2,1)}, bf16[512,1536]{1,0:T(8,128)(2,1)}, f32[384,1536]{1,0:T(8,128)}) custom-call(bf16[384,512]{1,0:T(8,128)(2,1)S(1)} %get-tuple-element.6.v_low, bf16[6,512,256]{2,1,0:T(8,128)(2,1)S(1)} %get-tuple-element.7.v_up, f32[6,384,256]{2,1,0:T(8,128)S(1)} %get-tuple-element.8.v_sch), custom_call_target="tpu_custom_call" | custom-call | tf_op jit(solution)/shard_map/pallas_call | solution.py:527

commit v3 on v2

--- a/solution.py
+++ b/solution.py
@@ -14,10 +14,12 @@
 NL = 4
 NR = 16
 NX = 4
+NZ = 8
 RB = 384
 PB = 32
 CB = 1536
 CW = 256
+HW = CW // 2
 NC = CB // CW
 OWN = RB // NL
 GAP = 4
@@ -69,7 +71,9 @@
     pst,
     rrecv,
     asum,
-    pvt,
+    single,
+    pair,
+    ppart,
     v_top,
     precv,
     s_tiles,
@@ -94,6 +98,8 @@
     l_rs,
     v_ss,
     v_rs,
+    y_ss,
+    y_rs,
 ):
     l = lax.axis_index("layer")
     r = lax.axis_index("row")
@@ -103,7 +109,9 @@
         return lax.rem(r + (2 * step + 2 * NR), NR)
 
     z_dev = {1: (l, row_of(1), x), -1: (l, row_of(-1), x)}
-    partner = (l, r + 1 - 2 * lax.rem(r, 2), x)
+    core = lax.rem(r, 2)
+    partner = (l, r + 1 - 2 * core, x)
+    own_pivots = pl.ds(pl.multiple_of(PB * (r // 2), PB), PB)
 
     def layer_of(d):
         return lax.rem(l + d, NL)
@@ -138,7 +146,7 @@
     load("anc", anc.at[pl.ds(pl.multiple_of(l * OWN, OWN), OWN), :], v_anc, 9)
 
     barrier = pltpu.get_barrier_semaphore()
-    others = [z_dev[1], z_dev[-1], partner]
+    others = [(l, row_of(d), x) for d in range(1, NZ)] + [partner]
     others += [(layer_of(d), r, x) for d in (1, 2, 3)]
     others += [(l, r, col_of(d)) for d in (1, 2, 3)]
     for dev in others:
@@ -195,8 +203,11 @@
 
     xc = {}
 
-    def onehot_rows(row_vector):
+    def onehot_rows(row_vector, by_core=False):
         rows = lax.broadcasted_iota(jnp.int32, (W, W), 0)
+        if by_core:
+            place = rows % (W // 2)
+            rows = 2 * PB * (place // PB) + PB * (rows // (W // 2)) + rows % PB
         return jnp.where(rows == row_vector, 1.0, 0.0).astype(BF)
 
     def times_t(a, b):
@@ -234,7 +245,7 @@
     def anc_left():
         loads["ali"].wait()
         loads["apiv"].wait()
-        v_alip[...] = times_t(v_ali[...], onehot_rows(v_apiv[...])).astype(BF)
+        v_alip[...] = times_t(v_ali[...], onehot_rows(v_apiv[...], True)).astype(BF)
 
     def ready(c):
         for i in range(8):
@@ -301,35 +312,92 @@
         qc[c, i] = send(ref, ref, q_ss.at[c, i], q_rs.at[c, i], partner)
 
     vc = {}
+    gc = {}
+    yc = {}
+    qc = {}
+    to_z = (4, 3, 5, 2, 6, 1, 7)
+
+    def along_z(n, ref):
+        for d in to_z:
+            gc[n, d] = send(ref, ref, p_ss.at[n, d - 1], p_rs.at[n, d - 1], (l, row_of(d), x))
+
+    def along_z_done(n):
+        for d in to_z:
+            gc[n, d].wait_recv()
+
+    def to_partner(n, ref):
+        qc[n] = send(ref, ref, q_ss.at[n], q_rs.at[n], partner)
+
+    def pair_piece(i, layer):
+        return 2 * i + layer // 2, pl.ds(pl.multiple_of(HW * lax.rem(layer, 2), HW), HW)
+
+    def pair_spread(i):
+        c, cols = pair_piece(i, l)
+        ppart[i, l] = pst[c, 0:PB, cols]
+        for d in (2, 1, 3):
+            to = layer_of(d)
+            c, cols = pair_piece(i, to)
+            vc[i, d] = send(
+                pst.at[c, pl.ds(0, PB), cols], ppart.at[i, l], v_ss.at[i, d - 1], v_rs.at[i, d - 1], (to, r, x)
+            )
+
+    def pair_sum(i):
+        if i == 0:
+            loads["top"].wait()
+        for d in (1, 2, 3):
+            vc[i, d].wait_recv()
+        total = v_top[:, pl.ds(pl.multiple_of(2 * CW * i + HW * l, HW), HW)]
+        for d in range(NL):
+            total = total + ppart[i, d].astype(F32)
+        pair[i, core, l, own_pivots, :] = total.astype(BF)
+        along_z(i, pair.at[i, core, l, own_pivots, :])
+
+    def pair_layers(i):
+        along_z_done(i)
+        ref = pair.at[i, core, l]
+        for d in (2, 1, 3):
+            yc[i, d] = send(ref, ref, y_ss.at[i, d - 1], y_rs.at[i, d - 1], (layer_of(d), r, x))
+
+    def pair_partner(i):
+        for d in (1, 2, 3):
+            yc[i, d].wait_recv()
+        to_partner(i, pair.at[i, core])
 
     def spread(c):
-        precv[c, l] = pst[c, 0:PB, :]
+        i = c - 2
+        precv[c - 4, l] = pst[c, 0:PB, :]
         for d in (2, 1, 3):
-            vc[c, d] = send(
-                pst.at[c, pl.ds(0, PB), :], precv.at[c, l], v_ss.at[c, d - 1], v_rs.at[c, d - 1], (layer_of(d), r, x)
+            vc[i, d] = send(
+                pst.at[c, pl.ds(0, PB), :], precv.at[c - 4, l], v_ss.at[i, d - 1], v_rs.at[i, d - 1], (layer_of(d), r, x)
             )
 
-    def pivots(c, hop):
-        if hop == 0:
-            if c == 0:
-                loads["top"].wait()
+    def single_sum(c):
+        for d in (1, 2, 3):
+            vc[c - 2, d].wait_recv()
+        total = v_top[:, c * CW : c * CW + CW]
+        for d in range(NL):
+            total = total + precv[c - 4, d].astype(F32)
+        single[c - 4, core, own_pivots, :] = total.astype(BF)
+        along_z(c - 2, single.at[c - 4, core, own_pivots, :])
+
+    def single_partner(c):
+        along_z_done(c - 2)
+        to_partner(c - 2, single.at[c - 4, core])
+
+    def gathered(c):
+        if c not in done:
+            done.add(c)
             for d in (1, 2, 3):
-                vc[c, d].wait_recv()
-            total = v_top[:, c * CW : c * CW + CW]
-            for d in range(NL):
-                total = total + precv[c, d].astype(F32)
-            pvt[c, block(r), :] = total.astype(BF)
-            p_send(c, 0, 1)
-            p_send(c, 0, -1)
-            q_send(c, 0, 0)
-            return
-        for dr in (1, -1):
-            if hop == 4 and dr < 0:
-                continue
-            pc[c, dr, hop - 1].wait_recv()
-            if hop < 3 or (hop == 3 and dr > 0):
-                p_send(c, hop, dr)
-            q_send(c, hop, dr)
+                ac[c, d].wait_recv()
+
+    def pivot_rows(c, of_core):
+        if c >= 4:
+            return single[c - 4, of_core]
+        i, e = c // 2, 2 * (c % 2)
+        return jnp.concatenate([pair[i, of_core, e], pair[i, of_core, e + 1]], axis=1)
+
+    done = set()
+    met = set()
 
     def anc_low():
         loads["aui"].wait()
@@ -365,10 +433,15 @@
                 low_copy(d).wait_send()
 
     def finish(c):
-        for i in range(8):
-            qc[c, i].wait_recv()
+        n = c // 2 if c < 4 else c - 2
+        if n not in met:
+            met.add(n)
+            qc[n].wait_recv()
         gathered(c)
-        v_up[c] = jnp.dot(v_alip[...], pvt[c], preferred_element_type=F32).astype(BF)
+        half = W // 2
+        up = jnp.dot(v_alip[:, 0:half], pivot_rows(c, 0), preferred_element_type=F32)
+        up = up + jnp.dot(v_alip[:, half:W], pivot_rows(c, 1), preferred_element_type=F32)
+        v_up[c] = up.astype(BF)
         prod = jnp.dot(v_low[...], v_up[c], preferred_element_type=F32)
         for p in range(3):
             tile = s_atiles[(3 * r + p) // 2, NC * x + c].astype(F32)
@@ -378,7 +451,10 @@
     def comp(c):
         ready(c)
         products(c, 0)
-        spread(c)
+        if c >= 4:
+            spread(c)
+        elif c % 2:
+            pair_spread(c // 2)
         products(c, 1)
         products(c, 2)
         scatter(c)
@@ -402,11 +478,12 @@
         at(PLACE[c, 3, 0] + GAP, z_last, c, 3)
     for c, g in ((0, 20), (1, 22), (2, 30), (3, 33)):
         at(g, comp, c)
-    for c, g in ((0, 25), (1, 27), (2, 34), (3, 37)):
-        at(g, pivots, c, 0)
+    for c, g in ((0, 25), (1, 27), (2, 34), (3, 38)):
         at(g, add_up, c)
-    for c, hop, g in ((0, 1, 32), (1, 1, 33), (0, 2, 38), (1, 2, 39)):
-        at(g, pivots, c, hop)
+    at(26, pair_sum, 0)
+    at(32, pair_layers, 0)
+    at(36, pair_partner, 0)
+    at(37, pair_sum, 1)
     at(31, anc_low)
 
     n = len(ORDER)
@@ -421,37 +498,21 @@
             if fn is z_last and args == (4, 3):
                 comp(4)
                 loads["atiles"].wait()
-    pivots(0, 3)
-    pivots(1, 3)
-    pivots(2, 1)
-    pivots(3, 1)
-    pivots(4, 0)
+    pair_layers(1)
+    single_sum(4)
     comp(5)
     add_up(4)
-    pivots(0, 4)
-    pivots(1, 4)
+    pair_partner(1)
     low_done()
     finish(0)
-    pivots(2, 2)
-    pivots(3, 2)
-    pivots(5, 0)
-    pivots(4, 1)
+    single_sum(5)
     add_up(5)
     finish(1)
-    pivots(2, 3)
-    pivots(3, 3)
-    pivots(5, 1)
-    pivots(4, 2)
-    pivots(2, 4)
-    pivots(3, 4)
     finish(2)
-    pivots(5, 2)
-    pivots(4, 3)
     finish(3)
-    pivots(4, 4)
-    pivots(5, 3)
+    single_partner(4)
     finish(4)
-    pivots(5, 4)
+    single_partner(5)
     finish(5)
     for cp in sent:
         cp.wait_send()
@@ -494,9 +555,11 @@
             vmem((NC, RB, CW), BF),
             vmem((NC, 3, OWN, CW), BF),
             vmem((NC, RB, CW), BF),
-            vmem((NC, W, CW), BF),
+            vmem((2, 2, W // 2, CW), BF),
+            vmem((2, 2, NL, W // 2, HW), BF),
+            vmem((2, NL, PB, HW), BF),
             vmem((PB, CB), F32),
-            vmem((NC, NL, PB, CW), BF),
+            vmem((2, NL, PB, CW), BF),
             pltpu.SMEM((LEAVES, 24, 24), jnp.int32),
             pltpu.SMEM((24, 24), jnp.int32),
             dma((11,)),
@@ -511,14 +574,16 @@
             dma((NC, 3)),
             dma((NC, 3)),
             dma((NC, 3)),
-            dma((NC, 2, 4)),
-            dma((NC, 2, 4)),
-            dma((NC, 8)),
-            dma((NC, 8)),
+            dma((4, NZ - 1)),
+            dma((4, NZ - 1)),
+            dma((4,)),
+            dma((4,)),
             dma((3,)),
             dma(()),
-            dma((NC, 3)),
-            dma((NC, 3)),
+            dma((4, 3)),
+            dma((4, 3)),
+            dma((2, 3)),
+            dma((2, 3)),
         ],
         compiler_params=pltpu.CompilerParams(
             collective_id=0, has_side_effects=True, vmem_limit_bytes=56 * 2**20

time: 104 us -> 97.8 us (0.940)
  Pallas kernels: 103 us -> 96.9 us
    pallas_call x1, Pallas kernels: 101 us -> 94.8 us  [shards(): pl.pallas_call(kernel, out_shape=(vmem((RB, W), BF), vmem((NC, W, CW), BF...]
where the time goes in v3:
time: 97.8 us; the launch traced here: 97.7 us
  Pallas kernels  96.9 us (99%)
    pallas_call x1, Pallas kernels, shards(): pl.pallas_call(kernel, out_shape=(vmem((RB, W), BF), vmem((NC, W, CW), BF...  94.8 us
    pallas_call x1, Pallas kernels, shards(): pl.pallas_call(write_out, out_shape=(jax.ShapeDtypeStruct((RB, W), BF), j...  2.15 us

profile of v3, /device:TPU:1, one launch (start us, length us, event | category | flops | bytes accessed | tf_op | source)
XLA Modules:
  0.0 97.7 jit_solution(7277772606422545992)
XLA Ops:
  0.6 94.8 %shard_map.130 = (bf16[384,512]{1,0:T(8,128)(2,1)S(1)}, bf16[6,512,256]{2,1,0:T(8,128)(2,1)S(1)}, f32[6,384,256]{2,1,0:T(8,128)S(1)}) custom-call(f32[384,1536]{1,0:T(8,128)} %anc.1, bf16[1,2,384,512]{3,2,1,0:T(8,128)(2,1)} %ll.1, bf16[1,8,32,1536]{3,2,1,0:T(8,128)(2,1)} %lu.1, bf16[1,2,512,512]{3,2,1,0:T(8,128)(2,1)} %lui.1, bf16[1,8,512,512]{3,2,1,0:T(8,128)(2,1)} %lli.1, ...), custom_call_target="tpu_custom_call" | custom-call | tf_op jit(solution)/shard_map/pallas_call | solution.py:537
  95.4 2.2 %shard_map.131 = (bf16[384,512]{1,0:T(8,128)(2,1)}, bf16[512,1536]{1,0:T(8,128)(2,1)}, f32[384,1536]{1,0:T(8,128)}) custom-call(bf16[384,512]{1,0:T(8,128)(2,1)S(1)} %get-tuple-element.6.v_low, bf16[6,512,256]{2,1,0:T(8,128)(2,1)S(1)} %get-tuple-element.7.v_up, f32[6,384,256]{2,1,0:T(8,128)S(1)} %get-tuple-element.8.v_sch), custom_call_target="tpu_custom_call" | custom-call | tf_op jit(solution)/shard_map/pallas_call | solution.py:592

commit v4 on v3

--- a/solution.py
+++ b/solution.py
@@ -20,25 +20,40 @@
 CB = 1536
 CW = 256
 HW = CW // 2
-NC = CB // CW
+WIDTHS = (256, 256, 256, 256, 256, 256)
+NC = len(WIDTHS)
+FIRST = [sum(WIDTHS[:c]) for c in range(NC)]
 OWN = RB // NL
-GAP = 4
+LAG = 3.0
 
 
 def ring_order():
     left = [(c, h, i) for c in range(NC) for h in range(4) for i in range(2) if h < 3 or i == 0]
-    order, place = [], {}
+    start, t = {}, 0.0
     while left:
-        g = len(order)
-        fit = [m for m in left if m[1] == 0 or place.get((m[0], m[1] - 1, m[2]), g) + GAP <= g]
-        order.append(fit[0] if fit else None)
+        fit = [
+            (c, h, i)
+            for c, h, i in left
+            if h == 0 or ((c, h - 1, i) in start and start[c, h - 1, i] + WIDTHS[c] / CW + LAG <= t)
+        ]
         if fit:
-            place[fit[0]] = g
+            start[fit[0]] = t
             left.remove(fit[0])
-    return order, place
-
-
-ORDER, PLACE = ring_order()
+            t += WIDTHS[fit[0][0]] / CW
+        else:
+            t += 0.25
+    return start
+
+
+START = ring_order()
+
+
+def spans(c):
+    return pl.ds(FIRST[c], WIDTHS[c])
+
+
+def span(c):
+    return pl.ds(0, WIDTHS[c])
 
 
 def kernel(
@@ -127,8 +142,8 @@
 
     for c in range(NC):
         cp = pltpu.make_async_copy(
-            lu.at[0, :, :, pl.ds(c * CW, CW)],
-            ubuf.at[c, :, pl.ds(pl.multiple_of(r * PB, PB), PB), :],
+            lu.at[0, :, :, spans(c)],
+            ubuf.at[c, :, pl.ds(pl.multiple_of(r * PB, PB), PB), span(c)],
             own_sem.at[c],
         )
         cp.start()
@@ -175,8 +190,8 @@
             if hop:
                 zc[c, dr, hop - 1, i].wait_recv()
             h = i if dr > 0 else 1 - i
-            dst = ubuf.at[c, pl.ds(4 * h, 4), block(row_of(-dr * hop)), :]
-            src = lu.at[0, pl.ds(4 * h, 4), :, pl.ds(c * CW, CW)] if hop == 0 else dst
+            dst = ubuf.at[c, pl.ds(4 * h, 4), block(row_of(-dr * hop)), span(c)]
+            src = lu.at[0, pl.ds(4 * h, 4), :, spans(c)] if hop == 0 else dst
             slot = 2 * hop + i
             zc[c, dr, hop, i] = send(src, dst, z_ss.at[c, n, slot], z_rs.at[c, n, slot], z_dev[dr])
         if hop == 0 and i == 0:
@@ -188,8 +203,8 @@
     def d_send(c, hop, dr):
         i = 0 if hop == 0 else (7 if hop == 4 else 2 * hop - 1 + (dr < 0))
         b = row_of(-dr * hop)
-        dst = ubuf.at[c, :, block(b), :]
-        src = lu.at[0, :, :, pl.ds(c * CW, CW)] if hop == 0 else dst
+        dst = ubuf.at[c, :, block(b), span(c)]
+        src = lu.at[0, :, :, spans(c)] if hop == 0 else dst
         dc[c, i] = send(src, dst, d_ss.at[c, i], d_rs.at[c, i], partner)
 
     def z_last(c, hop):
@@ -256,11 +271,11 @@
         rows = slice(128 * p, 128 * p + 128)
         total = None
         for k in range(LEAVES):
-            tile = s_tiles[k, (3 * r + p) // 2, NC * x + c].astype(F32)
-            prod = tile * jnp.dot(mbuf[k, rows, :], ubuf[c, k], preferred_element_type=F32)
+            tile = s_tiles[k, (3 * r + p) // 2, CB // TB * x + FIRST[c] // TB].astype(F32)
+            prod = tile * jnp.dot(mbuf[k, rows, :], ubuf[c, k, :, span(c)], preferred_element_type=F32)
             total = prod if total is None else total + prod
-        part[c, rows, :] = total
-        pst[c, rows, :] = total.astype(BF)
+        part[c, rows, span(c)] = total
+        pst[c, rows, span(c)] = total.astype(BF)
 
     rc = {}
     ac = {}
@@ -272,7 +287,11 @@
         for d in (2, 1, 3):
             to = layer_of(d)
             rc[c, d] = send(
-                pst.at[c, own_rows(to), :], rrecv.at[c, d - 1], r_ss.at[c, d - 1], r_rs.at[c, d - 1], (to, r, x)
+                pst.at[c, own_rows(to), span(c)],
+                rrecv.at[c, d - 1, :, span(c)],
+                r_ss.at[c, d - 1],
+                r_rs.at[c, d - 1],
+                (to, r, x),
             )
 
     def add_up(c):
@@ -280,36 +299,13 @@
             loads["anc"].wait()
         for d in (1, 2, 3):
             rc[c, d].wait_recv()
-        total = part[c, own_rows(l), :] + v_anc[:, c * CW : c * CW + CW]
+        total = part[c, own_rows(l), span(c)] + v_anc[:, spans(c)]
         for d in range(3):
-            total = total + rrecv[c, d].astype(F32)
-        asum[c, own_rows(l), :] = total.astype(BF)
-        ref = asum.at[c, own_rows(l), :]
+            total = total + rrecv[c, d, :, span(c)].astype(F32)
+        asum[c, own_rows(l), span(c)] = total.astype(BF)
+        ref = asum.at[c, own_rows(l), span(c)]
         for d in (2, 1, 3):
             ac[c, d] = send(ref, ref, a_ss.at[c, d - 1], a_rs.at[c, d - 1], (layer_of(d), r, x))
-
-    def gathered(c):
-        if c not in done:
-            done.add(c)
-            for d in (1, 2, 3):
-                ac[c, d].wait_recv()
-
-    done = set()
-
-    pc = {}
-    qc = {}
-
-    def p_send(c, hop, dr):
-        i = 0 if dr > 0 else 1
-        b = row_of(-dr * hop)
-        ref = pvt.at[c, block(b), :]
-        pc[c, dr, hop] = send(ref, ref, p_ss.at[c, i, hop], p_rs.at[c, i, hop], z_dev[dr])
-
-    def q_send(c, hop, dr):
-        i = 0 if hop == 0 else 2 * hop - 1 + (dr < 0)
-        b = row_of(-dr * hop)
-        ref = pvt.at[c, block(b), :]
-        qc[c, i] = send(ref, ref, q_ss.at[c, i], q_rs.at[c, i], partner)
 
     vc = {}
     gc = {}
@@ -350,10 +346,26 @@
         for d in range(NL):
             total = total + ppart[i, d].astype(F32)
         pair[i, core, l, own_pivots, :] = total.astype(BF)
-        along_z(i, pair.at[i, core, l, own_pivots, :])
+        if i == 0:
+            pair_hop(0)
+        else:
+            along_z(i, pair.at[i, core, l, own_pivots, :])
+
+    def pair_hop(hop):
+        for dr in (1, -1):
+            if hop == 4 and dr < 0:
+                continue
+            if hop:
+                gc[0, dr, hop - 1].wait_recv()
+            if hop < 3 or (hop == 3 and dr > 0):
+                at_z = lax.rem(r // 2 - dr * hop + NZ, NZ)
+                ref = pair.at[0, core, l, pl.ds(pl.multiple_of(PB * at_z, PB), PB), :]
+                slot = hop if dr > 0 else 4 + hop
+                gc[0, dr, hop] = send(ref, ref, p_ss.at[0, slot], p_rs.at[0, slot], z_dev[dr])
 
     def pair_layers(i):
-        along_z_done(i)
+        if i:
+            along_z_done(i)
         ref = pair.at[i, core, l]
         for d in (2, 1, 3):
             yc[i, d] = send(ref, ref, y_ss.at[i, d - 1], y_rs.at[i, d - 1], (layer_of(d), r, x))
@@ -365,24 +377,28 @@
 
     def spread(c):
         i = c - 2
-        precv[c - 4, l] = pst[c, 0:PB, :]
+        precv[c - 4, l, :, span(c)] = pst[c, 0:PB, span(c)]
         for d in (2, 1, 3):
             vc[i, d] = send(
-                pst.at[c, pl.ds(0, PB), :], precv.at[c - 4, l], v_ss.at[i, d - 1], v_rs.at[i, d - 1], (layer_of(d), r, x)
+                pst.at[c, pl.ds(0, PB), span(c)],
+                precv.at[c - 4, l, :, span(c)],
+                v_ss.at[i, d - 1],
+                v_rs.at[i, d - 1],
+                (layer_of(d), r, x),
             )
 
     def single_sum(c):
         for d in (1, 2, 3):
             vc[c - 2, d].wait_recv()
-        total = v_top[:, c * CW : c * CW + CW]
+        total = v_top[:, spans(c)]
         for d in range(NL):
-            total = total + precv[c - 4, d].astype(F32)
-        single[c - 4, core, own_pivots, :] = total.astype(BF)
-        along_z(c - 2, single.at[c - 4, core, own_pivots, :])
+            total = total + precv[c - 4, d, :, span(c)].astype(F32)
+        single[c - 4, core, own_pivots, span(c)] = total.astype(BF)
+        along_z(c - 2, single.at[c - 4, core, own_pivots, span(c)])
 
     def single_partner(c):
         along_z_done(c - 2)
-        to_partner(c - 2, single.at[c - 4, core])
+        to_partner(c - 2, single.at[c - 4, core, :, span(c)])
 
     def gathered(c):
         if c not in done:
@@ -392,7 +408,7 @@
 
     def pivot_rows(c, of_core):
         if c >= 4:
-            return single[c - 4, of_core]
+            return single[c - 4, of_core, :, span(c)]
         i, e = c // 2, 2 * (c % 2)
         return jnp.concatenate([pair[i, of_core, e], pair[i, of_core, e + 1]], axis=1)
 
@@ -441,32 +457,39 @@
         half = W // 2
         up = jnp.dot(v_alip[:, 0:half], pivot_rows(c, 0), preferred_element_type=F32)
         up = up + jnp.dot(v_alip[:, half:W], pivot_rows(c, 1), preferred_element_type=F32)
-        v_up[c] = up.astype(BF)
-        prod = jnp.dot(v_low[...], v_up[c], preferred_element_type=F32)
+        up = up.astype(BF)
+        v_up[c, :, span(c)] = up
+        prod = jnp.dot(v_low[...], up, preferred_element_type=F32)
         for p in range(3):
-            tile = s_atiles[(3 * r + p) // 2, NC * x + c].astype(F32)
+            tile = s_atiles[(3 * r + p) // 2, CB // TB * x + FIRST[c] // TB].astype(F32)
             rows = slice(128 * p, 128 * p + 128)
-            v_sch[c, rows, :] = asum[c, rows, :].astype(F32) - tile * prod[rows, :]
-
-    def comp(c):
+            v_sch[c, rows, span(c)] = asum[c, rows, span(c)].astype(F32) - tile * prod[rows, :]
+
+    def comp_top(c):
         ready(c)
         products(c, 0)
         if c >= 4:
             spread(c)
         elif c % 2:
             pair_spread(c // 2)
-        products(c, 1)
+
+    def comp_low(c):
         products(c, 2)
         scatter(c)
+
+    def comp(c):
+        comp_top(c)
+        products(c, 1)
+        comp_low(c)
 
     def m_ready():
         x_done()
         loads["tiles"].wait()
 
-    events = {}
-
-    def at(g, fn, *args):
-        events.setdefault(g, []).append((fn, args))
+    events = []
+
+    def at(t, fn, *args):
+        events.append((t, len(events), fn, args))
 
     at(1, left_factor, 0)
     at(2, left_factor, 1)
@@ -474,46 +497,53 @@
     at(10, x_relay)
     at(20, m_ready)
     for c in range(NC):
-        at(PLACE[c, 2, 1] + GAP, z_last, c, 2)
-        at(PLACE[c, 3, 0] + GAP, z_last, c, 3)
-    for c, g in ((0, 20), (1, 22), (2, 30), (3, 33)):
-        at(g, comp, c)
-    for c, g in ((0, 25), (1, 27), (2, 34), (3, 38)):
-        at(g, add_up, c)
-    at(26, pair_sum, 0)
-    at(32, pair_layers, 0)
-    at(36, pair_partner, 0)
-    at(37, pair_sum, 1)
-    at(31, anc_low)
-
-    n = len(ORDER)
-    for g in range(n):
-        if ORDER[g] is not None:
-            z_send(*ORDER[g])
-        for fn, args in events.pop(g, []):
+        end = WIDTHS[c] / CW + LAG
+        at(max(START[c, 2, 1] + end, START[c, 3, 0]), z_last, c, 2)
+        at(START[c, 3, 0] + end, z_last, c, 3)
+        if 4 <= c < NC - 1:
+            at(START[c, 3, 0] + end, comp, c)
+            at(START[c, 3, 0] + end + 2.5, single_sum, c)
+            at(START[c, 3, 0] + end + 4, add_up, c)
+    for c, t in ((0, 20), (1, 22), (2, START[2, 3, 0] + 1 + LAG), (3, START[3, 3, 0] + 1 + LAG)):
+        at(t, comp_top, c)
+        at(t + 1, products, c, 1)
+        at(t + 2, comp_low, c)
+    for c, t in ((0, 27), (1, 29), (2, 35), (3, 38)):
+        at(t, add_up, c)
+    at(26.5, pair_sum, 0)
+    for hop in range(1, 5):
+        at(26.5 + 3.5 * hop, pair_hop, hop)
+    at(40.5, pair_layers, 0)
+    at(43.5, pair_partner, 0)
+    at(36, pair_sum, 1)
+    at(43.2, pair_layers, 1)
+    at(34, anc_low)
+    at(40, loads["atiles"].wait)
+    events.sort()
+    ready_at = START[NC - 1, 3, 0] + WIDTHS[NC - 1] / CW + LAG
+
+    def until(t):
+        while events and events[0][0] <= t:
+            _, _, fn, args = events.pop(0)
             fn(*args)
-    for g in sorted(events):
-        for fn, args in events[g]:
-            fn(*args)
-            if fn is z_last and args == (4, 3):
-                comp(4)
-                loads["atiles"].wait()
-    pair_layers(1)
-    single_sum(4)
-    comp(5)
-    add_up(4)
-    pair_partner(1)
+
+    for message, t in sorted(START.items(), key=lambda m: m[1]):
+        z_send(*message)
+        until(t)
+    until(ready_at)
+    comp(NC - 1)
+    until(100)
     low_done()
     finish(0)
-    single_sum(5)
-    add_up(5)
+    single_sum(NC - 1)
+    pair_partner(1)
     finish(1)
     finish(2)
+    add_up(NC - 1)
     finish(3)
-    single_partner(4)
-    finish(4)
-    single_partner(5)
-    finish(5)
+    for c in range(4, NC):
+        single_partner(c)
+        finish(c)
     for cp in sent:
         cp.wait_send()
 
@@ -521,9 +551,9 @@
 def write_out(v_low, v_up, v_sch, o_low, o_up, o_sch, sem):
     copies = [pltpu.make_async_copy(v_low, o_low, sem.at[2 * NC])]
     for c in range(NC):
-        cols = pl.ds(c * CW, CW)
-        copies.append(pltpu.make_async_copy(v_sch.at[c], o_sch.at[:, cols], sem.at[c]))
-        copies.append(pltpu.make_async_copy(v_up.at[c], o_up.at[:, cols], sem.at[NC + c]))
+        cols, own = spans(c), span(c)
+        copies.append(pltpu.make_async_copy(v_sch.at[c, :, own], o_sch.at[:, cols], sem.at[c]))
+        copies.append(pltpu.make_async_copy(v_up.at[c, :, own], o_up.at[:, cols], sem.at[NC + c]))
     for cp in copies:
         cp.start()
     for cp in copies:
@@ -555,11 +585,11 @@
             vmem((NC, RB, CW), BF),
             vmem((NC, 3, OWN, CW), BF),
             vmem((NC, RB, CW), BF),
-            vmem((2, 2, W // 2, CW), BF),
+            vmem((NC - 4, 2, W // 2, CW), BF),
             vmem((2, 2, NL, W // 2, HW), BF),
             vmem((2, NL, PB, HW), BF),
             vmem((PB, CB), F32),
-            vmem((2, NL, PB, CW), BF),
+            vmem((NC - 4, NL, PB, CW), BF),
             pltpu.SMEM((LEAVES, 24, 24), jnp.int32),
             pltpu.SMEM((24, 24), jnp.int32),
             dma((11,)),
@@ -574,14 +604,14 @@
             dma((NC, 3)),
             dma((NC, 3)),
             dma((NC, 3)),
-            dma((4, NZ - 1)),
-            dma((4, NZ - 1)),
-            dma((4,)),
-            dma((4,)),
+            dma((NC - 2, NZ - 1)),
+            dma((NC - 2, NZ - 1)),
+            dma((NC - 2,)),
+            dma((NC - 2,)),
             dma((3,)),
             dma(()),
-            dma((4, 3)),
-            dma((4, 3)),
+            dma((NC - 2, 3)),
+            dma((NC - 2, 3)),
             dma((2, 3)),
             dma((2, 3)),
         ],

time: 97.8 us -> 96.2 us (0.984)
  Pallas kernels: 96.9 us -> 95.3 us
    pallas_call x1, Pallas kernels: 94.8 us -> 93.1 us  [shards(): pl.pallas_call(kernel, out_shape=(vmem((RB, W), BF), vmem((NC, W, CW), BF...]
where the time goes in v4:
time: 96.2 us; the launch traced here: 96.1 us
  Pallas kernels  95.3 us (99%)
    pallas_call x1, Pallas kernels, shards(): pl.pallas_call(kernel, out_shape=(vmem((RB, W), BF), vmem((NC, W, CW), BF...  93.1 us
    pallas_call x1, Pallas kernels, shards(): pl.pallas_call(write_out, out_shape=(jax.ShapeDtypeStruct((RB, W), BF), j...  2.15 us

profile of v4, /device:TPU:1, one launch (start us, length us, event | category | flops | bytes accessed | tf_op | source)
XLA Modules:
  0.0 96.1 jit_solution(4541339047135483259)
XLA Ops:
  0.6 93.1 %shard_map.130 = (bf16[384,512]{1,0:T(8,128)(2,1)S(1)}, bf16[6,512,256]{2,1,0:T(8,128)(2,1)S(1)}, f32[6,384,256]{2,1,0:T(8,128)S(1)}) custom-call(f32[384,1536]{1,0:T(8,128)} %anc.1, bf16[1,2,384,512]{3,2,1,0:T(8,128)(2,1)} %ll.1, bf16[1,8,32,1536]{3,2,1,0:T(8,128)(2,1)} %lu.1, bf16[1,2,512,512]{3,2,1,0:T(8,128)(2,1)} %lui.1, bf16[1,8,512,512]{3,2,1,0:T(8,128)(2,1)} %lli.1, ...), custom_call_target="tpu_custom_call" | custom-call | tf_op jit(solution)/shard_map/pallas_call | solution.py:567
  93.8 2.2 %shard_map.131 = (bf16[384,512]{1,0:T(8,128)(2,1)}, bf16[512,1536]{1,0:T(8,128)(2,1)}, f32[384,1536]{1,0:T(8,128)}) custom-call(bf16[384,512]{1,0:T(8,128)(2,1)S(1)} %get-tuple-element.6.v_low, bf16[6,512,256]{2,1,0:T(8,128)(2,1)S(1)} %get-tuple-element.7.v_up, f32[6,384,256]{2,1,0:T(8,128)S(1)} %get-tuple-element.8.v_sch), custom_call_target="tpu_custom_call" | custom-call | tf_op jit(solution)/shard_map/pallas_call | solution.py:622

commit v5 on v4

--- a/solution.py
+++ b/solution.py
@@ -134,6 +134,13 @@
     def col_of(d):
         return lax.rem(x + d + NX, NX)
 
+    barrier = pltpu.get_barrier_semaphore()
+    others = [(l, row_of(d), x) for d in range(1, NZ)] + [partner]
+    others += [(layer_of(d), r, x) for d in (1, 2, 3)]
+    others += [(l, r, col_of(d)) for d in (1, 2, 3)]
+    for dev in others:
+        pl.semaphore_signal(barrier, inc=1, device_id=dev, device_id_type=MESH)
+
     loads = {}
 
     def load(name, src, dst, index):
@@ -160,12 +167,6 @@
     load("top", anc.at[pl.ds(0, PB), :], v_top, 10)
     load("anc", anc.at[pl.ds(pl.multiple_of(l * OWN, OWN), OWN), :], v_anc, 9)
 
-    barrier = pltpu.get_barrier_semaphore()
-    others = [(l, row_of(d), x) for d in range(1, NZ)] + [partner]
-    others += [(layer_of(d), r, x) for d in (1, 2, 3)]
-    others += [(l, r, col_of(d)) for d in (1, 2, 3)]
-    for dev in others:
-        pl.semaphore_signal(barrier, inc=1, device_id=dev, device_id_type=MESH)
     pl.semaphore_wait(barrier, len(others))
 
     sent = []
@@ -453,13 +454,13 @@
         if n not in met:
             met.add(n)
             qc[n].wait_recv()
-        gathered(c)
         half = W // 2
         up = jnp.dot(v_alip[:, 0:half], pivot_rows(c, 0), preferred_element_type=F32)
         up = up + jnp.dot(v_alip[:, half:W], pivot_rows(c, 1), preferred_element_type=F32)
         up = up.astype(BF)
         v_up[c, :, span(c)] = up
         prod = jnp.dot(v_low[...], up, preferred_element_type=F32)
+        gathered(c)
         for p in range(3):
             tile = s_atiles[(3 * r + p) // 2, CB // TB * x + FIRST[c] // TB].astype(F32)
             rows = slice(128 * p, 128 * p + 128)
@@ -491,9 +492,9 @@
     def at(t, fn, *args):
         events.append((t, len(events), fn, args))
 
-    at(1, left_factor, 0)
-    at(2, left_factor, 1)
-    at(5, anc_left)
+    at(3, left_factor, 0)
+    at(3, left_factor, 1)
+    at(7, anc_left)
     at(10, x_relay)
     at(20, m_ready)
     for c in range(NC):

time: 96.2 us -> 96.1 us (level)
  no operation moved by 1% of the time
where the time goes in v5:
time: 96.1 us; the launch traced here: 96 us
  Pallas kernels  95.2 us (99%)
    pallas_call x1, Pallas kernels, shards(): pl.pallas_call(kernel, out_shape=(vmem((RB, W), BF), vmem((NC, W, CW), BF...  93.1 us
    pallas_call x1, Pallas kernels, shards(): pl.pallas_call(write_out, out_shape=(jax.ShapeDtypeStruct((RB, W), BF), j...  2.15 us

profile of v5, /device:TPU:1, one launch (start us, length us, event | category | flops | bytes accessed | tf_op | source)
XLA Modules:
  0.0 96.0 jit_solution(3097753694837983945)
XLA Ops:
  0.6 93.1 %shard_map.130 = (bf16[384,512]{1,0:T(8,128)(2,1)S(1)}, bf16[6,512,256]{2,1,0:T(8,128)(2,1)S(1)}, f32[6,384,256]{2,1,0:T(8,128)S(1)}) custom-call(f32[384,1536]{1,0:T(8,128)} %anc.1, bf16[1,2,384,512]{3,2,1,0:T(8,128)(2,1)} %ll.1, bf16[1,8,32,1536]{3,2,1,0:T(8,128)(2,1)} %lu.1, bf16[1,2,512,512]{3,2,1,0:T(8,128)(2,1)} %lui.1, bf16[1,8,512,512]{3,2,1,0:T(8,128)(2,1)} %lli.1, ...), custom_call_target="tpu_custom_call" | custom-call | tf_op jit(solution)/shard_map/pallas_call | solution.py:568
  93.7 2.2 %shard_map.131 = (bf16[384,512]{1,0:T(8,128)(2,1)}, bf16[512,1536]{1,0:T(8,128)(2,1)}, f32[384,1536]{1,0:T(8,128)}) custom-call(bf16[384,512]{1,0:T(8,128)(2,1)S(1)} %get-tuple-element.6.v_low, bf16[6,512,256]{2,1,0:T(8,128)(2,1)S(1)} %get-tuple-element.7.v_up, f32[6,384,256]{2,1,0:T(8,128)S(1)} %get-tuple-element.8.v_sch), custom_call_target="tpu_custom_call" | custom-call | tf_op jit(solution)/shard_map/pallas_call | solution.py:623
